TPU v7x, 32 devices: a whole 2x2x4 slice. The times are simulated.
32 devices in a mesh: tm: 4 (over z), gx: 4 (over y, x), gy: 2 (over core).
Axes of the slice: x: 2, y: 2, z: 4, core: 2. Of those that a mesh axis runs over, the one named last changes fastest.
Arguments:
- guesses: float32 [4, 64, 32, 256], P('tm', None, 'gx', 'gy'), may hold values from -6 to 6
- forcing: float32 [4, 64, 32, 256], P('tm', None, 'gx', 'gy'), may hold values from -4 to 4
- step_weight: float32 [16], replicated, may hold values from 0.25 to 1
- land_mask: int32 [32, 256], P('gx', 'gy'), may hold values 0 or 1
- fine_matrix: float32 [64, 64], replicated, may hold values from -1 to 1
- coupling: float32 [4, 64, 64], replicated, may hold values from -0.09375 to 0.09375
- coarse_matrix: float32 [64, 64], replicated, may hold values from -1 to 1
Outputs:
- updated_points: float32 [4, 64, 32, 256], P('tm', None, 'gx', 'gy')
- residual: float32 [4, 64, 32, 256], P('tm', None, 'gx', 'gy')
All inputs are finite; a program needn't handle non-finite values. No bound on the sum of `land_mask` on one device may be relied on, other than what follows from the above.
Results may differ from a plain program's by a relative error of at most 0.0003.
Values sent between devices are 32-bit elements; how exact they have to be, the bound alone decides.
No kernel may reach another device: no remote copies, remote signals or barrier semaphores. Data moves between devices by JAX's collectives and lax.ppermute only.
A program may use at most 64 MiB of HBM per device.

v0:
```python
import jax
import jax.numpy as jnp
from jax import lax
from jax.experimental import pallas as pl
from jax.experimental.pallas import tpu as pltpu
from jax.sharding import PartitionSpec as P

F32 = jnp.float32
LANES = 128


def lane_of(shape):
    return lax.broadcasted_iota(jnp.int32, shape, len(shape) - 1)


def roll(value, shift, axis=1):
    shift %= value.shape[axis]
    return value if shift == 0 else pltpu.roll(value, shift, axis)


class Plan:
    def __init__(self, mesh_sizes, dof, rows, cols, steps):
        self.planes, self.gx, self.gy = mesh_sizes
        self.dof, self.rows, self.cols, self.halo = dof, rows, cols, steps
        self.strip = cols // self.gx
        self.window = self.strip + 2 * steps
        self.pack = LANES // self.window
        self.groups = rows // self.pack
        self.width = self.gx * self.window
        self.back = LANES // self.strip
        self.back_groups = rows // self.back
        assert self.gy == 2 and cols == LANES and self.window * self.pack == LANES
        assert rows * self.halo == LANES and rows == 8 and self.width % LANES == 0
        assert self.strip >= self.halo and self.back_groups * self.back == rows


def call(kernel, outs, n_in, smem=(), scratch=()):
    specs = [
        pl.BlockSpec(memory_space=pltpu.SMEM if i in smem else pltpu.VMEM) for i in range(n_in)
    ]
    out_specs = [pl.BlockSpec(memory_space=pltpu.VMEM) for _ in outs]
    single = len(outs) == 1
    return pl.pallas_call(
        kernel,
        in_specs=specs,
        out_specs=out_specs[0] if single else out_specs,
        out_shape=outs[0] if single else outs,
        scratch_shapes=list(scratch),
    )


def edge_kernel(plan):
    h, n = plan.halo, plan.cols

    def packed(row_of, half):
        lane = lane_of((1, LANES))
        result = None
        for x in range(plan.rows):
            row = row_of(x)
            low = roll(row, h * x)
            high = roll(row, h * x - (n - h))
            piece = jnp.where(half == 0, high, low)
            result = piece if x == 0 else jnp.where(lane >= h * x, piece, result)
        return result

    def kernel(half_ref, forcing_ref, guess_ref, land_ref, edge_f_ref, edge_g_ref):
        half = half_ref[0]
        edge_f_ref[0 : plan.dof] = packed(lambda x: forcing_ref[0, :, x, :], half)
        edge_f_ref[plan.dof :] = land_ref[...].astype(F32)
        edge_g_ref[...] = packed(lambda x: guess_ref[0, :, x, :], half)

    return call(
        kernel,
        [
            jax.ShapeDtypeStruct((plan.dof + plan.rows, LANES), F32),
            jax.ShapeDtypeStruct((plan.dof, LANES), F32),
        ],
        4,
        smem=(0,),
    )


def windows(plan, row, below, above):
    h = plan.halo
    lane = lane_of((1, LANES))
    found = []
    for q in range(plan.gx):
        source = row
        if q == 0:
            source = jnp.where(lane >= LANES - h, below, source)
        if q == plan.gx - 1:
            source = jnp.where(lane < h, above, source)
        found.append((source, h - plan.strip * q))
    return found


def pack_kernel(plan, with_land):
    h, w = plan.halo, plan.window

    def kernel(half_ref, field_ref, edge_ref, *rest):
        half = half_ref[0]
        out_ref = rest[-1]
        lane = lane_of((1, LANES))
        edge = edge_ref[0 : plan.dof]
        below_edge = jnp.where(half == 1, edge, 0.0)
        above_edge = jnp.where(half == 0, edge, 0.0)

        def of_row(x):
            below = roll(below_edge, LANES - h - h * x)
            above = roll(above_edge, -h * x)
            return windows(plan, field_ref[0, :, x, :], below, above)

        for j in range(plan.groups):
            parts = [of_row(j + plan.groups * m) for m in range(plan.pack)]
            for q in range(plan.gx):
                piece = None
                for m in range(plan.pack):
                    source, shift = parts[m][q]
                    moved = roll(source, shift + w * m)
                    piece = moved if m == 0 else jnp.where(lane >= w * m, moved, piece)
                out_ref[q, plan.dof * j : plan.dof * (j + 1)] = piece
        if with_land:
            land = rest[0][...].astype(F32)
            other = edge_ref[plan.dof :]
            below = jnp.where(half == 1, other, 0.0)
            above = jnp.where(half == 0, other, 0.0)
            for q, (source, shift) in enumerate(windows(plan, land, below, above)):
                piece = None
                for m in range(plan.pack):
                    moved = roll(roll(source, shift + w * m), -plan.groups * m, 0)
                    piece = moved if m == 0 else jnp.where(lane >= w * m, moved, piece)
                out_ref[q, plan.dof * plan.groups :] = piece

    extra = plan.rows if with_land else 0
    shape = (plan.gx, plan.dof * plan.groups + extra, LANES)
    return call(kernel, [jax.ShapeDtypeStruct(shape, F32)], 4 if with_land else 3, smem=(0,))


def relax_kernel(plan, steps):
    dof, w, rows, h = plan.dof, plan.window, plan.rows, plan.halo
    vregs = plan.width // LANES
    per = LANES // w

    def assembled(piece_ref, j, row0, count):
        m = j // plan.groups
        base = row0 + count * (j % plan.groups)
        lane = lane_of((1, LANES))
        halves = []
        for v in range(vregs):
            value = None
            for u in range(per):
                part = piece_ref[v * per + u, base : base + count]
                part = roll(part, w * (u - m))
                value = part if u == 0 else jnp.where(lane >= w * u, part, value)
            halves.append(value)
        return jnp.concatenate(halves, axis=1)

    def kernel(weight_ref, matrix_ref, f_ref, a_ref, out_ref, state_ref, f_all, mask_all, acc, wst, est):
        lane = lane_of((1, plan.width))

        def put(slot, j, value):
            high = value.astype(jnp.bfloat16)
            low = (value - high.astype(F32)).astype(jnp.bfloat16)
            state_ref[slot, j, 0:dof] = high
            state_ref[slot, j, dof : 2 * dof] = low

        for j in range(rows):
            put(0, j, assembled(a_ref, j, 0, dof))
            f_all[j] = assembled(f_ref, j, 0, dof)
            mask_all[j] = jnp.broadcast_to(
                assembled(f_ref, j, dof * plan.groups, 1), (8, plan.width)
            )

        def rolled(value, shift):
            parts = [
                roll(value[:, LANES * v : LANES * (v + 1)], shift) for v in range(vregs)
            ]
            return jnp.concatenate(parts, axis=1)

        def step(slot, weight, finish):
            for j in range(rows):
                high = state_ref[slot, j, 0:dof]
                both = state_ref[slot, j]
                out = jnp.dot(
                    matrix_ref[...],
                    jnp.concatenate([both, high], axis=0),
                    preferred_element_type=F32,
                )
                wst[j] = out[dof : 2 * dof]
                est[j] = out[2 * dof : 3 * dof]
                acc[j] = (
                    out[0:dof]
                    + rolled(out[3 * dof : 4 * dof], 1)
                    + rolled(out[4 * dof : 5 * dof], -1)
                )
            for j in range(rows):
                if j > 0:
                    west = wst[j - 1]
                else:
                    west = jnp.where(lane >= w, pltpu.roll(wst[rows - 1], w, 1), 0.0)
                if j < rows - 1:
                    east = est[j + 1]
                else:
                    east = jnp.where(
                        lane < plan.width - w, pltpu.roll(est[0], plan.width - w, 1), 0.0
                    )
                total = acc[j] + west + east + weight * f_all[j]
                finish(j, total * mask_all[j, 0:1])

        def two(i, carry):
            k = steps - 1 - 2 * i
            step(0, weight_ref[k], lambda j, v: put(1, j, v))
            step(1, weight_ref[k - 1], lambda j, v: put(0, j, v))
            return carry

        lax.fori_loop(0, steps // 2 - 1, two, 0)
        step(0, weight_ref[1], lambda j, v: put(1, j, v))

        def emit(j, value):
            f_all[j] = value

        step(1, weight_ref[0], emit)
        s = plan.strip
        small = lane_of((1, LANES))
        for q in range(plan.gx):
            v, u = divmod(q, per)
            for group in range(plan.back_groups):
                piece = None
                for m in range(plan.back):
                    part = f_all[group * plan.back + m, :, LANES * v : LANES * (v + 1)]
                    part = roll(part, s * m - (w * u + h))
                    piece = part if m == 0 else jnp.where(small >= s * m, part, piece)
                out_ref[q, dof * group : dof * (group + 1)] = piece

    tile = (rows, dof, plan.width)
    return call(
        kernel,
        [jax.ShapeDtypeStruct((plan.gx, dof * plan.back_groups, LANES), F32)],
        4,
        smem=(0,),
        scratch=[
            pltpu.VMEM((2, rows, 2 * dof, plan.width), jnp.bfloat16),
            pltpu.VMEM(tile, F32),
            pltpu.VMEM((rows, 8, plan.width), F32),
            pltpu.VMEM(tile, F32),
            pltpu.VMEM(tile, F32),
            pltpu.VMEM(tile, F32),
        ],
    )


def residual_kernel(plan):
    dof, s = plan.dof, plan.strip

    def kernel(piece_ref, guess_ref, land_ref, out_ref):
        lane = lane_of((1, LANES))
        mask = land_ref[...].astype(F32)
        for x in range(plan.rows):
            group, m = divmod(x, plan.back)
            row = None
            for q in range(plan.gx):
                part = roll(piece_ref[q, dof * group : dof * (group + 1)], s * (q - m))
                row = part if q == 0 else jnp.where(lane >= s * q, part, row)
            out_ref[0, :, x, :] = row - guess_ref[0, :, x, :] * mask[x : x + 1]

    shape = (1, dof, plan.rows, LANES)
    return call(kernel, [jax.ShapeDtypeStruct(shape, F32)], 3)


def stacked_matrix(fine_matrix, coupling):
    full = jnp.concatenate([fine_matrix[None], coupling], axis=0)
    full = full.reshape(-1, full.shape[-1])
    rounded = lax.reduce_precision(full, 8, 7)
    high = rounded.astype(jnp.bfloat16)
    low = (full - rounded).astype(jnp.bfloat16)
    return jnp.concatenate([high, high, low], axis=1)


def earlier(count):
    return [(t, t - 1) for t in range(1, count)]


def per_device(guesses, forcing, step_weight, land_mask, fine_matrix, coupling, coarse_matrix):
    planes, gx, gy = (lax.axis_size(name) for name in ("tm", "gx", "gy"))
    _, dof, rows, cols = guesses.shape
    steps = step_weight.shape[0]
    plan = Plan((planes, gx, gy), dof, rows, cols, steps)
    half = lax.axis_index("gy").astype(jnp.int32)[None]

    start = lax.ppermute(guesses, "tm", earlier(planes))
    edge_f, edge_g = edge_kernel(plan)(half, forcing, guesses, land_mask)
    edge_f = lax.ppermute(edge_f, "gy", [(0, 1), (1, 0)])
    edge_g = lax.ppermute(
        edge_g,
        ("tm", "gy"),
        [(t * gy + c, (t - 1) * gy + 1 - c) for t in range(1, planes) for c in range(gy)],
    )
    f_pieces = pack_kernel(plan, True)(half, forcing, edge_f, land_mask)
    f_pieces = lax.all_to_all(f_pieces, "gx", 0, 0, tiled=True)
    a_pieces = pack_kernel(plan, False)(half, start, edge_g)
    a_pieces = lax.all_to_all(a_pieces, "gx", 0, 0, tiled=True)
    relaxed = relax_kernel(plan, steps)(
        step_weight, stacked_matrix(fine_matrix, coupling), f_pieces, a_pieces
    )
    relaxed = lax.all_to_all(relaxed, "gx", 0, 0, tiled=True)
    residual = residual_kernel(plan)(relaxed, guesses, land_mask)

    mask = land_mask.astype(F32)[None]

    def advance(field):
        moved = jnp.einsum("ij,jxy->ixy", coarse_matrix, field, precision=lax.Precision.HIGHEST)
        return moved * mask + residual[0]

    def turn(_, incoming):
        return lax.ppermute(advance(incoming), "tm", earlier(planes))

    incoming = lax.fori_loop(0, planes - 1, turn, jnp.zeros_like(residual[0]))
    return guesses + advance(incoming)[None], residual


def solution(mesh):
    return jax.shard_map(
        per_device,
        mesh=mesh,
        in_specs=(
            P("tm", None, "gx", "gy"),
            P("tm", None, "gx", "gy"),
            P(),
            P("gx", "gy"),
            P(),
            P(),
            P(),
        ),
        out_specs=(P("tm", None, "gx", "gy"), P("tm", None, "gx", "gy")),
        check_vma=False,
    )
```

profile of v0, /device:TPU:0, one launch (start us, length us, event | category | flops | bytes accessed | tf_op | source)
XLA Modules:
  0.0 97.8 jit_solution(9358883923696806195)
XLA Ops:
  0.6 2.0 %shard_map.86 = (f32[72,128]{1,0:T(8,128)}, f32[64,128]{1,0:T(8,128)}) custom-call(s32[1]{0:T(128)} %bitcast.6.half_ref, f32[1,64,8,128]{3,2,1,0:T(8,128)} %field_ref.1, f32[1,64,8,128]{3,2,1,0:T(8,128)} %guess_ref.3, s32[8,128]{1,0:T(8,128)} %land_ref.3), custom_call_target="tpu_custom_call" | custom-call | tf_op jit(solution)/shard_map/pallas_call | solution.py:291
  2.6 0.5 collective-permute-start.1
  3.1 1.1 %collective-permute-done.1.edge_ref = f32[72,128]{1,0:T(8,128)S(1)} collective-permute-done((f32[72,128]{1,0:T(8,128)}, f32[72,128]{1,0:T(8,128)S(1)}, u32[]{:S(2)}, u32[]{:S(2)}) %collective-permute-start.1) | collective-permute-done | bytes 36896 | tf_op jit(solution)/shard_map/ppermute | solution.py:292
  4.2 0.0 copy-start.10
  4.2 0.6 copy-done.10
  4.8 2.4 %shard_map.87 = f32[4,264,128]{2,1,0:T(8,128)} custom-call(s32[1]{0:T(128)} %bitcast.6.half_ref, f32[1,64,8,128]{3,2,1,0:T(8,128)} %field_ref.1, f32[72,128]{1,0:T(8,128)} %copy-done.10, s32[8,128]{1,0:T(8,128)} %land_ref.3), custom_call_target="tpu_custom_call" | custom-call | tf_op jit(solution)/shard_map/pallas_call | solution.py:298
  7.2 0.0 copy-start
  7.2 0.0 copy-start.13
  7.2 5.2 %all-to-all-start = ((f32[4,264,128]{2,1,0:T(8,128)}), f32[4,264,128]{2,1,0:T(8,128)S(1)}, u32[]{:S(2)}, u32[]{:S(2)}) async-start(f32[4,264,128]{2,1,0:T(8,128)} %shard_map.87), calls=%async_computation | async-start | bytes 1081344 | tf_op jit(solution)/shard_map/all_to_all | solution.py:299
  12.4 0.0 copy-done
  12.4 1.3 %collective-permute-start.2 = (f32[1,64,8,128]{3,2,1,0:T(8,128)S(1)}, f32[1,64,8,128]{3,2,1,0:T(8,128)S(1)}, u32[]{:S(2)}, u32[]{:S(2)}) collective-permute-start(f32[1,64,8,128]{3,2,1,0:T(8,128)S(1)} %copy-done), channel_id=1, source_target_pairs={{8,0},{16,8},{24,16},{9,1},{17,9},{25,17},{10,2},{18,10},{26,18},{... | collective-permute-start | bytes 786440 | tf_op jit(solution)/shard_map/ppermute | solution.py:290
  13.7 0.0 copy-done.13
  13.7 1.3 %collective-permute-start.3 = (f32[64,128]{1,0:T(8,128)S(1)}, f32[64,128]{1,0:T(8,128)S(1)}, u32[]{:S(2)}, u32[]{:S(2)}) collective-permute-start(f32[64,128]{1,0:T(8,128)S(1)} %copy-done.13), channel_id=1, source_target_pairs={{8,1},{9,0},{16,9},{17,8},{24,17},{25,16},{10,3},{11,2},{18,11},{1... | collective-permute-start | bytes 98312 | tf_op jit(solution)/shard_map/ppermute | solution.py:293
  15.0 7.0 %collective-permute-done.3.edge_ref = f32[64,128]{1,0:T(8,128)S(1)} collective-permute-done((f32[64,128]{1,0:T(8,128)S(1)}, f32[64,128]{1,0:T(8,128)S(1)}, u32[]{:S(2)}, u32[]{:S(2)}) %collective-permute-start.3) | collective-permute-done | bytes 32800 | tf_op jit(solution)/shard_map/ppermute | solution.py:293
  22.0 0.0 copy-start.12
  22.0 0.7 collective-permute-done.2.field_ref
  22.7 0.0 copy-done.12
  22.7 0.0 copy-start.7
  22.7 0.7 copy-done.7
  23.4 2.4 %shard_map.88 = f32[4,256,128]{2,1,0:T(8,128)} custom-call(s32[1]{0:T(128)} %bitcast.6.half_ref, f32[1,64,8,128]{3,2,1,0:T(8,128)} %copy-done.7, f32[64,128]{1,0:T(8,128)} %copy-done.12), custom_call_target="tpu_custom_call" | custom-call | tf_op jit(solution)/shard_map/pallas_call | solution.py:300
  25.8 0.0 copy-start.8
  25.8 0.0 copy-start.11
  25.8 0.0 all-to-all-done.f_ref
  25.8 0.0 copy-start.3
  25.8 4.1 %all-to-all-start.1 = ((f32[4,256,128]{2,1,0:T(8,128)}), f32[4,256,128]{2,1,0:T(8,128)S(1)}, u32[]{:S(2)}, u32[]{:S(2)}) async-start(f32[4,256,128]{2,1,0:T(8,128)} %shard_map.88), calls=%async_computation.1 | async-start | bytes 1048576 | tf_op jit(solution)/shard_map/all_to_all | solution.py:301
  29.9 0.0 copy-done.8
  29.9 0.0 copy-done.11
  29.9 0.0 copy-done.3
  29.9 0.8 pad_maximum_fusion.1.matrix_ref
  30.7 8.1 %all-to-all-done.1.a_ref = f32[4,256,128]{2,1,0:T(8,128)S(1)} async-done(((f32[4,256,128]{2,1,0:T(8,128)}), f32[4,256,128]{2,1,0:T(8,128)S(1)}, u32[]{:S(2)}, u32[]{:S(2)}) %all-to-all-start.1) | async-done | bytes 524320 | tf_op jit(solution)/shard_map/all_to_all | solution.py:301
  38.8 0.0 copy-start.4
  38.8 0.8 copy-done.4
  39.7 16.4 %shard_map.89 = f32[4,128,128]{2,1,0:T(8,128)} custom-call(f32[16]{0:T(128)} %weight_ref.1, bf16[320,192]{1,0:T(8,128)(2,1)} %pad_maximum_fusion.1.matrix_ref, f32[4,264,128]{2,1,0:T(8,128)} %copy-done.3, f32[4,256,128]{2,1,0:T(8,128)} %copy-done.4), custom_call_target="tpu_custom_call" | custom-call | tf_op jit(solution)/shard_map/pallas_call | solution.py:302
  56.1 0.0 copy-start.9
  56.1 3.5 %all-to-all-start.2 = ((f32[4,128,128]{2,1,0:T(8,128)}), f32[4,128,128]{2,1,0:T(8,128)S(1)}, u32[]{:S(2)}, u32[]{:S(2)}) async-start(f32[4,128,128]{2,1,0:T(8,128)} %shard_map.89), calls=%async_computation.2 | async-start | bytes 524288 | tf_op jit(solution)/shard_map/all_to_all | solution.py:305
  59.6 0.0 copy-done.9
  59.6 5.4 %all-to-all-done.2.piece_ref = f32[4,128,128]{2,1,0:T(8,128)S(1)} async-done(((f32[4,128,128]{2,1,0:T(8,128)}), f32[4,128,128]{2,1,0:T(8,128)S(1)}, u32[]{:S(2)}, u32[]{:S(2)}) %all-to-all-start.2) | async-done | bytes 262176 | tf_op jit(solution)/shard_map/all_to_all | solution.py:305
  65.0 0.0 copy-start.6
  65.0 0.7 copy-done.6
  65.7 2.1 %shard_map.90 = f32[1,64,8,128]{3,2,1,0:T(8,128)} custom-call(f32[4,128,128]{2,1,0:T(8,128)} %copy-done.6, f32[1,64,8,128]{3,2,1,0:T(8,128)} %guess_ref.3, s32[8,128]{1,0:T(8,128)} %land_ref.3), custom_call_target="tpu_custom_call" | custom-call | tf_op jit(solution)/shard_map/pallas_call | solution.py:306
  67.8 1.0 %copy.9 = f32[1,64,8,128]{3,1,2,0:T(8,128)S(1)} copy(f32[1,64,8,128]{3,2,1,0:T(8,128)} %shard_map.90) | data formatting | bytes 524288 | tf_op jit(solution)/shard_map/while | solution.py:317
  68.8 0.0 copy-start.5
  68.8 0.7 copy-done.5
  69.6 26.3 %while.10 = (s32[]{:T(128)}, f32[64,8,128]{2,0,1:T(8,128)S(1)}, f32[64,64]{1,0:T(8,128)S(1)}, f32[1,8,128]{2,1,0:T(8,128)S(1)}, f32[1,64,8,128]{3,1,2,0:T(8,128)S(1)}, /*index=5*/s32[]{:T(128)}) while((s32[]{:T(128)}, f32[64,8,128]{2,0,1:T(8,128)S(1)}, f32[64,64]{1,0:T(8,128)S(1)}, f32[1,8,128]{2,1,0:T(8,128)S(1)}, ...), condition=%wide.region_1.0_spmd, body=%wide.region_0.0_spmd.sunk | while | flops 50462720 | bytes 1855597 | solution.py:317
  69.6 0.4 fusion.13
  69.9 1.3 %collective-permute-start = (f32[64,8,128]{2,0,1:T(8,128)S(1)}, f32[64,8,128]{2,0,1:T(8,128)S(1)}, u32[]{:S(2)}, u32[]{:S(2)}) collective-permute-start(f32[64,8,128]{2,0,1:T(8,128)S(1)} %fusion.13), channel_id=1, source_target_pairs={{8,0},{16,8},{24,16},{9,1},{17,9},{25,17},{10,2},{18,10},{26,18},{... | collective-permute-start | bytes 786440 | tf_op jit(solution)/shard_map/while/body/eval_jaxpr/ppermute | solution.py:315
  71.2 7.4 %collective-permute-done = f32[64,8,128]{2,0,1:T(8,128)S(1)} collective-permute-done((f32[64,8,128]{2,0,1:T(8,128)S(1)}, f32[64,8,128]{2,0,1:T(8,128)S(1)}, u32[]{:S(2)}, u32[]{:S(2)}) %collective-permute-start) | collective-permute-done | bytes 262176 | tf_op jit(solution)/shard_map/while/body/eval_jaxpr/ppermute | solution.py:315
  78.6 0.4 fusion.13
  79.0 1.3 %collective-permute-start = (f32[64,8,128]{2,0,1:T(8,128)S(1)}, f32[64,8,128]{2,0,1:T(8,128)S(1)}, u32[]{:S(2)}, u32[]{:S(2)}) collective-permute-start(f32[64,8,128]{2,0,1:T(8,128)S(1)} %fusion.13), channel_id=1, source_target_pairs={{8,0},{16,8},{24,16},{9,1},{17,9},{25,17},{10,2},{18,10},{26,18},{... | collective-permute-start | bytes 786440 | tf_op jit(solution)/shard_map/while/body/eval_jaxpr/ppermute | solution.py:315
  80.3 7.0 %collective-permute-done = f32[64,8,128]{2,0,1:T(8,128)S(1)} collective-permute-done((f32[64,8,128]{2,0,1:T(8,128)S(1)}, f32[64,8,128]{2,0,1:T(8,128)S(1)}, u32[]{:S(2)}, u32[]{:S(2)}) %collective-permute-start) | collective-permute-done | bytes 262176 | tf_op jit(solution)/shard_map/while/body/eval_jaxpr/ppermute | solution.py:315
  87.3 0.4 fusion.13
  87.6 1.3 %collective-permute-start = (f32[64,8,128]{2,0,1:T(8,128)S(1)}, f32[64,8,128]{2,0,1:T(8,128)S(1)}, u32[]{:S(2)}, u32[]{:S(2)}) collective-permute-start(f32[64,8,128]{2,0,1:T(8,128)S(1)} %fusion.13), channel_id=1, source_target_pairs={{8,0},{16,8},{24,16},{9,1},{17,9},{25,17},{10,2},{18,10},{26,18},{... | collective-permute-start | bytes 786440 | tf_op jit(solution)/shard_map/while/body/eval_jaxpr/ppermute | solution.py:315
  89.0 7.0 %collective-permute-done = f32[64,8,128]{2,0,1:T(8,128)S(1)} collective-permute-done((f32[64,8,128]{2,0,1:T(8,128)S(1)}, f32[64,8,128]{2,0,1:T(8,128)S(1)}, u32[]{:S(2)}, u32[]{:S(2)}) %collective-permute-start) | collective-permute-done | bytes 262176 | tf_op jit(solution)/shard_map/while/body/eval_jaxpr/ppermute | solution.py:315
  95.9 0.0 copy-start.1
  95.9 0.0 copy-start.2
  95.9 0.4 fusion.3
  96.3 0.6 copy-done.1
  96.9 0.1 copy-done.2
  96.9 0.9 bitcast_add_fusion
  (4 shorter events, 0.1 us)
Async XLA Ops:
  2.6 1.6 %collective-permute-start.1 = (f32[72,128]{1,0:T(8,128)}, f32[72,128]{1,0:T(8,128)S(1)}, u32[]{:S(2)}, u32[]{:S(2)}) collective-permute-start(f32[72,128]{1,0:T(8,128)} %get-tuple-element.31), channel_id=1, source_target_pairs={{0,1},{1,0},{2,3},{3,2},{4,5},{5,4},{6,7},{7,6},{8,9},{9,8},{10,11... | collective-permute-start | bytes 110600 | tf_op jit(solution)/shard_map/ppermute | solution.py:292
  4.2 0.6 copy-start.10
  7.2 5.2 %copy-start = (f32[1,64,8,128]{3,2,1,0:T(8,128)S(1)}, f32[1,64,8,128]{3,2,1,0:T(8,128)}, u32[]{:S(2)}) copy-start(f32[1,64,8,128]{3,2,1,0:T(8,128)} %guess_ref.3) | copy-start | bytes 786436
  7.2 6.5 %copy-start.13 = (f32[64,128]{1,0:T(8,128)S(1)}, f32[64,128]{1,0:T(8,128)}, u32[]{:S(2)}) copy-start(f32[64,128]{1,0:T(8,128)} %get-tuple-element.32) | copy-start | bytes 98308
  7.2 18.6 %all-to-all-start = ((f32[4,264,128]{2,1,0:T(8,128)}), f32[4,264,128]{2,1,0:T(8,128)S(1)}, u32[]{:S(2)}, u32[]{:S(2)}) async-start(f32[4,264,128]{2,1,0:T(8,128)} %shard_map.87), calls=%async_computation | async-start | bytes 1081344 | tf_op jit(solution)/shard_map/all_to_all | solution.py:299
  12.4 10.3 %collective-permute-start.2 = (f32[1,64,8,128]{3,2,1,0:T(8,128)S(1)}, f32[1,64,8,128]{3,2,1,0:T(8,128)S(1)}, u32[]{:S(2)}, u32[]{:S(2)}) collective-permute-start(f32[1,64,8,128]{3,2,1,0:T(8,128)S(1)} %copy-done), channel_id=1, source_target_pairs={{8,0},{16,8},{24,16},{9,1},{17,9},{25,17},{10,2},{18,10},{26,18},{... | collective-permute-start | bytes 786440 | tf_op jit(solution)/shard_map/ppermute | solution.py:290
  13.7 8.3 %collective-permute-start.3 = (f32[64,128]{1,0:T(8,128)S(1)}, f32[64,128]{1,0:T(8,128)S(1)}, u32[]{:S(2)}, u32[]{:S(2)}) collective-permute-start(f32[64,128]{1,0:T(8,128)S(1)} %copy-done.13), channel_id=1, source_target_pairs={{8,1},{9,0},{16,9},{17,8},{24,17},{25,16},{10,3},{11,2},{18,11},{1... | collective-permute-start | bytes 98312 | tf_op jit(solution)/shard_map/ppermute | solution.py:293
  22.0 0.7 copy-start.12
  22.7 0.7 copy-start.7
  25.8 4.1 %copy-start.8 = (f32[4,64,64]{2,1,0:T(8,128)S(1)}, f32[4,64,64]{2,1,0:T(8,128)}, u32[]{:S(2)}) copy-start(f32[4,64,64]{2,1,0:T(8,128)} %param.14) | copy-start | bytes 196612
  25.8 4.1 %copy-start.11 = (f32[64,64]{1,0:T(8,128)S(1)}, f32[64,64]{1,0:T(8,128)}, u32[]{:S(2)}) copy-start(f32[64,64]{1,0:T(8,128)} %param.13) | copy-start | bytes 49156
  25.8 4.1 %copy-start.3 = (f32[4,264,128]{2,1,0:T(8,128)}, f32[4,264,128]{2,1,0:T(8,128)S(1)}, u32[]{:S(2)}) copy-start(f32[4,264,128]{2,1,0:T(8,128)S(1)} %all-to-all-done.f_ref) | copy-start | bytes 1622020
  25.8 13.0 %all-to-all-start.1 = ((f32[4,256,128]{2,1,0:T(8,128)}), f32[4,256,128]{2,1,0:T(8,128)S(1)}, u32[]{:S(2)}, u32[]{:S(2)}) async-start(f32[4,256,128]{2,1,0:T(8,128)} %shard_map.88), calls=%async_computation.1 | async-start | bytes 1048576 | tf_op jit(solution)/shard_map/all_to_all | solution.py:301
  38.8 0.8 copy-start.4
  56.1 3.6 %copy-start.9 = (s32[8,128]{1,0:T(8,128)S(1)}, s32[8,128]{1,0:T(8,128)}, u32[]{:S(2)}) copy-start(s32[8,128]{1,0:T(8,128)} %land_ref.3) | copy-start | bytes 12292
  56.1 9.0 %all-to-all-start.2 = ((f32[4,128,128]{2,1,0:T(8,128)}), f32[4,128,128]{2,1,0:T(8,128)S(1)}, u32[]{:S(2)}, u32[]{:S(2)}) async-start(f32[4,128,128]{2,1,0:T(8,128)} %shard_map.89), calls=%async_computation.2 | async-start | bytes 524288 | tf_op jit(solution)/shard_map/all_to_all | solution.py:305
  65.0 0.7 copy-start.6
  68.8 0.8 copy-start.5
  69.9 8.7 %collective-permute-start = (f32[64,8,128]{2,0,1:T(8,128)S(1)}, f32[64,8,128]{2,0,1:T(8,128)S(1)}, u32[]{:S(2)}, u32[]{:S(2)}) collective-permute-start(f32[64,8,128]{2,0,1:T(8,128)S(1)} %fusion.13), channel_id=1, source_target_pairs={{8,0},{16,8},{24,16},{9,1},{17,9},{25,17},{10,2},{18,10},{26,18},{... | collective-permute-start | bytes 786440 | tf_op jit(solution)/shard_map/while/body/eval_jaxpr/ppermute | solution.py:315
  79.0 8.3 %collective-permute-start = (f32[64,8,128]{2,0,1:T(8,128)S(1)}, f32[64,8,128]{2,0,1:T(8,128)S(1)}, u32[]{:S(2)}, u32[]{:S(2)}) collective-permute-start(f32[64,8,128]{2,0,1:T(8,128)S(1)} %fusion.13), channel_id=1, source_target_pairs={{8,0},{16,8},{24,16},{9,1},{17,9},{25,17},{10,2},{18,10},{26,18},{... | collective-permute-start | bytes 786440 | tf_op jit(solution)/shard_map/while/body/eval_jaxpr/ppermute | solution.py:315
  87.6 8.3 %collective-permute-start = (f32[64,8,128]{2,0,1:T(8,128)S(1)}, f32[64,8,128]{2,0,1:T(8,128)S(1)}, u32[]{:S(2)}, u32[]{:S(2)}) collective-permute-start(f32[64,8,128]{2,0,1:T(8,128)S(1)} %fusion.13), channel_id=1, source_target_pairs={{8,0},{16,8},{24,16},{9,1},{17,9},{25,17},{10,2},{18,10},{26,18},{... | collective-permute-start | bytes 786440 | tf_op jit(solution)/shard_map/while/body/eval_jaxpr/ppermute | solution.py:315
  95.9 1.0 copy-start.1
  95.9 1.0 %copy-start.2 = (f32[1,64,8,128]{3,2,1,0:T(8,128)S(1)}, f32[1,64,8,128]{3,2,1,0:T(8,128)}, u32[]{:S(2)}) copy-start(f32[1,64,8,128]{3,2,1,0:T(8,128)} %shard_map.90) | copy-start | bytes 786436
where the time goes:
time: 98.5 us; the launch traced here: 97.8 us
  waiting for transfers between devices  43.6 us (44%)
  Pallas kernels  25.2 us (26%)
  starting transfers between devices  19.7 us (20%)
  local copies, waits for them, and re-layouts  5.26 us (5%)
  other arithmetic  1.7 us (2%)
  matrix products  1.45 us (1%)
    ppermute x3, waiting for transfers between devices, turn(): return lax.ppermute(advance(incoming), 'tm', earlier(planes))  21.3 us
    pallas_call x1, Pallas kernels, per_device(): relax_kernel(plan, steps)  16.4 us
    all_to_all x1, waiting for transfers between devices, per_device(): a_pieces = lax.all_to_all(a_pieces, 'gx', 0, 0, tiled=True)  8.11 us
    ppermute x1, waiting for transfers between devices, per_device(): lax.ppermute(edge_g, ('tm', 'gy'), [(t * gy + c, (t - 1) * gy + 1 - c) fo...  6.99 us
    all_to_all x1, waiting for transfers between devices, per_device(): relaxed = lax.all_to_all(relaxed, 'gx', 0, 0, tiled=True)  5.39 us
    all_to_all x1, starting transfers between devices, per_device(): f_pieces = lax.all_to_all(f_pieces, 'gx', 0, 0, tiled=True)  5.18 us
    unnamed x28, local copies, waits for them, and re-layouts  4.24 us
    all_to_all x1, starting transfers between devices, per_device(): a_pieces = lax.all_to_all(a_pieces, 'gx', 0, 0, tiled=True)  4.06 us
  transfers between devices with their start and end apart: 9, of which 8 were waited for; matrix products, arithmetic and copies ran while one was open for 1% of the time, Pallas kernels for 2%

commit v1 on v0

--- a/solution.py
+++ b/solution.py
@@ -4,6 +4,7 @@
 from jax.experimental import pallas as pl
 from jax.experimental.pallas import tpu as pltpu
 from jax.sharding import PartitionSpec as P
+
 
 F32 = jnp.float32
 LANES = 128
@@ -29,24 +30,39 @@
         self.width = self.gx * self.window
         self.back = LANES // self.strip
         self.back_groups = rows // self.back
+        self.square = self.planes == self.gx
         assert self.gy == 2 and cols == LANES and self.window * self.pack == LANES
+        assert self.gx & (self.gx - 1) == 0 and steps % 2 == 0
         assert rows * self.halo == LANES and rows == 8 and self.width % LANES == 0
         assert self.strip >= self.halo and self.back_groups * self.back == rows
 
 
-def call(kernel, outs, n_in, smem=(), scratch=()):
+def call(kernel, outs, n_in, smem=(), scratch=(), leave=(), hbm=()):
     specs = [
         pl.BlockSpec(memory_space=pltpu.SMEM if i in smem else pltpu.VMEM) for i in range(n_in)
     ]
     out_specs = [pl.BlockSpec(memory_space=pltpu.VMEM) for _ in outs]
+    outs = [
+        out if i in leave else pltpu.VMEM(out.shape, out.dtype) for i, out in enumerate(outs)
+    ]
     single = len(outs) == 1
-    return pl.pallas_call(
+    run = pl.pallas_call(
         kernel,
         in_specs=specs,
         out_specs=out_specs[0] if single else out_specs,
         out_shape=outs[0] if single else outs,
         scratch_shapes=list(scratch),
     )
+
+    def placed(*args):
+        return run(
+            *(
+                arg if i in smem or i in hbm else pltpu.with_memory_space_constraint(arg, pltpu.VMEM)
+                for i, arg in enumerate(args)
+            )
+        )
+
+    return placed
 
 
 def edge_kernel(plan):
@@ -63,8 +79,8 @@
             result = piece if x == 0 else jnp.where(lane >= h * x, piece, result)
         return result
 
-    def kernel(half_ref, forcing_ref, guess_ref, land_ref, edge_f_ref, edge_g_ref):
-        half = half_ref[0]
+    def kernel(place_ref, forcing_ref, guess_ref, land_ref, edge_f_ref, edge_g_ref):
+        half = place_ref[2]
         edge_f_ref[0 : plan.dof] = packed(lambda x: forcing_ref[0, :, x, :], half)
         edge_f_ref[plan.dof :] = land_ref[...].astype(F32)
         edge_g_ref[...] = packed(lambda x: guess_ref[0, :, x, :], half)
@@ -77,6 +93,7 @@
         ],
         4,
         smem=(0,),
+        hbm=(1, 2, 3),
     )
 
 
@@ -94,14 +111,19 @@
     return found
 
 
+def sides(shape, count):
+    return [jax.ShapeDtypeStruct(shape, F32) for _ in range(count)]
+
+
 def pack_kernel(plan, with_land):
-    h, w = plan.halo, plan.window
-
-    def kernel(half_ref, field_ref, edge_ref, *rest):
-        half = half_ref[0]
-        out_ref = rest[-1]
+    h, w, dof = plan.halo, plan.window, plan.dof
+    base = dof * plan.groups
+
+    def kernel(place_ref, field_ref, edge_ref, *rest):
+        half = place_ref[2]
+        outs, all_ref = rest[-1 - plan.gx : -1], rest[-1]
         lane = lane_of((1, LANES))
-        edge = edge_ref[0 : plan.dof]
+        edge = edge_ref[0:dof]
         below_edge = jnp.where(half == 1, edge, 0.0)
         above_edge = jnp.where(half == 0, edge, 0.0)
 
@@ -118,10 +140,11 @@
                     source, shift = parts[m][q]
                     moved = roll(source, shift + w * m)
                     piece = moved if m == 0 else jnp.where(lane >= w * m, moved, piece)
-                out_ref[q, plan.dof * j : plan.dof * (j + 1)] = piece
+                all_ref[q, dof * j : dof * (j + 1)] = piece
         if with_land:
-            land = rest[0][...].astype(F32)
-            other = edge_ref[plan.dof :]
+            land_ref, guess_ref = rest[0], rest[1]
+            land = land_ref[...].astype(F32)
+            other = edge_ref[dof:]
             below = jnp.where(half == 1, other, 0.0)
             above = jnp.where(half == 0, other, 0.0)
             for q, (source, shift) in enumerate(windows(plan, land, below, above)):
@@ -129,34 +152,62 @@
                 for m in range(plan.pack):
                     moved = roll(roll(source, shift + w * m), -plan.groups * m, 0)
                     piece = moved if m == 0 else jnp.where(lane >= w * m, moved, piece)
-                out_ref[q, plan.dof * plan.groups :] = piece
-
-    extra = plan.rows if with_land else 0
-    shape = (plan.gx, plan.dof * plan.groups + extra, LANES)
-    return call(kernel, [jax.ShapeDtypeStruct(shape, F32)], 4 if with_land else 3, smem=(0,))
+                all_ref[q, base : base + plan.rows] = piece
+            for group in range(plan.back_groups):
+                start = base + plan.rows + dof * group
+                for q in range(plan.gx):
+                    piece = None
+                    for m in range(plan.back):
+                        part = roll(
+                            guess_ref[0, :, group * plan.back + m, :], plan.strip * (m - q)
+                        )
+                        piece = part if m == 0 else jnp.where(lane >= plan.strip * m, part, piece)
+                    all_ref[q, start : start + dof] = piece
+        for k in range(plan.gx):
+            outs[k][...] = all_ref[place_ref[1] ^ k]
+
+    extra = plan.rows + dof * plan.back_groups if with_land else 0
+    shape = (base + extra, LANES)
+    return call(
+        kernel,
+        sides(shape, plan.gx),
+        5 if with_land else 3,
+        smem=(0,),
+        scratch=[pltpu.VMEM((plan.gx,) + shape, F32)],
+    )
 
 
 def relax_kernel(plan, steps):
-    dof, w, rows, h = plan.dof, plan.window, plan.rows, plan.halo
+    dof, w, rows, h, gx, s = plan.dof, plan.window, plan.rows, plan.halo, plan.gx, plan.strip
     vregs = plan.width // LANES
     per = LANES // w
-
-    def assembled(piece_ref, j, row0, count):
+    base = dof * plan.groups
+
+    def assembled(piece_of, j, row0, count):
         m = j // plan.groups
-        base = row0 + count * (j % plan.groups)
+        first = row0 + count * (j % plan.groups)
         lane = lane_of((1, LANES))
         halves = []
         for v in range(vregs):
             value = None
             for u in range(per):
-                part = piece_ref[v * per + u, base : base + count]
+                part = piece_of(v * per + u)[first : first + count]
                 part = roll(part, w * (u - m))
                 value = part if u == 0 else jnp.where(lane >= w * u, part, value)
             halves.append(value)
         return jnp.concatenate(halves, axis=1)
 
-    def kernel(weight_ref, matrix_ref, f_ref, a_ref, out_ref, state_ref, f_all, mask_all, acc, wst, est):
+    def kernel(place_ref, weight_ref, matrix_ref, *refs):
+        f_in, a_in, refs = refs[:gx], refs[gx : 2 * gx], refs[2 * gx :]
+        home, across, land_ref, refs = (
+            refs[:gx],
+            refs[gx : gx + plan.gx],
+            refs[2 * gx],
+            refs[2 * gx + 1 :],
+        )
+        state_ref, f_all, mask_all, acc, wst, est, f_raw, a_raw, r_all, land_all = refs
         lane = lane_of((1, plan.width))
+        small = lane_of((1, LANES))
 
         def put(slot, j, value):
             high = value.astype(jnp.bfloat16)
@@ -164,11 +215,14 @@
             state_ref[slot, j, 0:dof] = high
             state_ref[slot, j, dof : 2 * dof] = low
 
+        for k in range(gx):
+            f_raw[place_ref[1] ^ k] = f_in[k][...]
+            a_raw[place_ref[1] ^ k] = a_in[k][...]
         for j in range(rows):
-            put(0, j, assembled(a_ref, j, 0, dof))
-            f_all[j] = assembled(f_ref, j, 0, dof)
+            put(0, j, assembled(lambda q: a_raw.at[q], j, 0, dof))
+            f_all[j] = assembled(lambda q: f_raw.at[q], j, 0, dof)
             mask_all[j] = jnp.broadcast_to(
-                assembled(f_ref, j, dof * plan.groups, 1), (8, plan.width)
+                assembled(lambda q: f_raw.at[q], j, base, 1), (8, plan.width)
             )
 
         def rolled(value, shift):
@@ -220,24 +274,38 @@
             f_all[j] = value
 
         step(1, weight_ref[0], emit)
-        s = plan.strip
-        small = lane_of((1, LANES))
-        for q in range(plan.gx):
+        for q in range(gx):
             v, u = divmod(q, per)
+            lanes = slice(LANES * v, LANES * (v + 1))
             for group in range(plan.back_groups):
                 piece = None
+                land = None
                 for m in range(plan.back):
-                    part = f_all[group * plan.back + m, :, LANES * v : LANES * (v + 1)]
-                    part = roll(part, s * m - (w * u + h))
+                    j = group * plan.back + m
+                    shift = s * m - (w * u + h)
+                    part = roll(f_all[j, :, lanes], shift)
+                    mask = roll(mask_all[j, :, lanes], shift)
                     piece = part if m == 0 else jnp.where(small >= s * m, part, piece)
-                out_ref[q, dof * group : dof * (group + 1)] = piece
+                    land = mask if m == 0 else jnp.where(small >= s * m, mask, land)
+                start = base + rows + dof * group
+                guess = f_raw[q, start : start + dof]
+                r_all[q, dof * group : dof * (group + 1)] = piece - guess * land[0:1]
+                land_all[q, 8 * group : 8 * (group + 1)] = land
+        for k in range(gx):
+            home[k][...] = r_all[place_ref[1] ^ k]
+        if plan.square:
+            for k in range(gx):
+                across[k][...] = r_all[place_ref[0] ^ k]
+            land_ref[...] = land_all[place_ref[0]]
 
     tile = (rows, dof, plan.width)
+    piece = (dof * plan.back_groups, LANES)
+    extra = rows + dof * plan.back_groups
     return call(
         kernel,
-        [jax.ShapeDtypeStruct((plan.gx, dof * plan.back_groups, LANES), F32)],
-        4,
-        smem=(0,),
+        sides(piece, 2 * gx) + sides((8 * plan.back_groups, LANES), 1),
+        3 + 2 * gx,
+        smem=(0, 1),
         scratch=[
             pltpu.VMEM((2, rows, 2 * dof, plan.width), jnp.bfloat16),
             pltpu.VMEM(tile, F32),
@@ -245,31 +313,106 @@
             pltpu.VMEM(tile, F32),
             pltpu.VMEM(tile, F32),
             pltpu.VMEM(tile, F32),
+            pltpu.VMEM((gx, base + extra, LANES), F32),
+            pltpu.VMEM((gx, base, LANES), F32),
+            pltpu.VMEM((gx,) + piece, F32),
+            pltpu.VMEM((gx, 8 * plan.back_groups, LANES), F32),
         ],
     )
 
 
+def unpacked(plan, pieces, x, lane):
+    group, m = divmod(x, plan.back)
+    row = None
+    for q in range(plan.gx):
+        part = pieces[q, plan.dof * group : plan.dof * (group + 1)]
+        part = roll(part, plan.strip * (q - m))
+        row = part if q == 0 else jnp.where(lane >= plan.strip * q, part, row)
+    return row
+
+
 def residual_kernel(plan):
-    dof, s = plan.dof, plan.strip
-
-    def kernel(piece_ref, guess_ref, land_ref, out_ref):
+    def kernel(place_ref, guess_ref, *refs):
+        out_ref, sum_ref, all_ref = refs[-3:]
         lane = lane_of((1, LANES))
-        mask = land_ref[...].astype(F32)
+        for k in range(plan.gx):
+            all_ref[place_ref[1] ^ k] = refs[k][...]
         for x in range(plan.rows):
-            group, m = divmod(x, plan.back)
-            row = None
-            for q in range(plan.gx):
-                part = roll(piece_ref[q, dof * group : dof * (group + 1)], s * (q - m))
-                row = part if q == 0 else jnp.where(lane >= s * q, part, row)
-            out_ref[0, :, x, :] = row - guess_ref[0, :, x, :] * mask[x : x + 1]
-
-    shape = (1, dof, plan.rows, LANES)
-    return call(kernel, [jax.ShapeDtypeStruct(shape, F32)], 3)
-
-
-def stacked_matrix(fine_matrix, coupling):
-    full = jnp.concatenate([fine_matrix[None], coupling], axis=0)
-    full = full.reshape(-1, full.shape[-1])
+            row = unpacked(plan, all_ref, x, lane)
+            out_ref[0, :, x, :] = row
+            sum_ref[0, :, x, :] = guess_ref[0, :, x, :] + row
+
+    shape = (1, plan.dof, plan.rows, LANES)
+    return call(
+        kernel,
+        sides(shape, 2),
+        2 + plan.gx,
+        smem=(0,),
+        leave=(0,),
+        scratch=[pltpu.VMEM((plan.gx, plan.dof * plan.back_groups, LANES), F32)],
+    )
+
+
+def coarse_kernel(plan):
+    dof, n = plan.dof, plan.back_groups
+
+    def kernel(place_ref, matrix_ref, land_ref, *refs):
+        outs, r_all, e_all = refs[plan.planes : -2], refs[-2], refs[-1]
+        for k in range(plan.planes):
+            r_all[place_ref[0] ^ k] = refs[k][...]
+        e_all[plan.planes - 1] = jnp.zeros_like(e_all[0])
+        carry = None
+        for t in range(plan.planes - 2, -1, -1):
+            fresh = [r_all[t + 1, dof * v : dof * (v + 1)] for v in range(n)]
+            if carry is not None:
+                fresh = [a + b for a, b in zip(fresh, carry)]
+            value = jnp.concatenate(fresh, axis=1)
+            high = value.astype(jnp.bfloat16)
+            low = (value - high.astype(F32)).astype(jnp.bfloat16)
+            moved = jnp.dot(
+                matrix_ref[...],
+                jnp.concatenate([high, low, high], axis=0),
+                preferred_element_type=F32,
+            )
+            carry = []
+            for v in range(n):
+                part = moved[:, LANES * v : LANES * (v + 1)] * land_ref[8 * v : 8 * v + 1]
+                e_all[t, dof * v : dof * (v + 1)] = part
+                carry.append(part)
+        for k in range(plan.gx):
+            outs[k][...] = e_all[place_ref[1] ^ k]
+
+    piece = (dof * n, LANES)
+    return call(
+        kernel,
+        sides(piece, plan.gx),
+        3 + plan.planes,
+        smem=(0,),
+        scratch=[pltpu.VMEM((plan.planes,) + piece, F32)] * 2,
+    )
+
+
+def update_kernel(plan):
+    def kernel(place_ref, sum_ref, *refs):
+        out_ref, all_ref = refs[-2:]
+        lane = lane_of((1, LANES))
+        for k in range(plan.gx):
+            all_ref[place_ref[0] ^ k] = refs[k][...]
+        for x in range(plan.rows):
+            out_ref[0, :, x, :] = sum_ref[0, :, x, :] + unpacked(plan, all_ref, x, lane)
+
+    shape = (1, plan.dof, plan.rows, LANES)
+    return call(
+        kernel,
+        sides(shape, 1),
+        2 + plan.gx,
+        smem=(0,),
+        leave=(0,),
+        scratch=[pltpu.VMEM((plan.gx, plan.dof * plan.back_groups, LANES), F32)],
+    )
+
+
+def split_matrix(full):
     rounded = lax.reduce_precision(full, 8, 7)
     high = rounded.astype(jnp.bfloat16)
     low = (full - rounded).astype(jnp.bfloat16)
@@ -278,6 +421,14 @@
 
 def earlier(count):
     return [(t, t - 1) for t in range(1, count)]
+
+
+def swapped(pieces, axis):
+    count = lax.axis_size(axis)
+    return [pieces[0]] + [
+        lax.ppermute(pieces[k], axis, [(i, i ^ k) for i in range(count)])
+        for k in range(1, count)
+    ]
 
 
 def per_device(guesses, forcing, step_weight, land_mask, fine_matrix, coupling, coarse_matrix):
@@ -285,37 +436,51 @@
     _, dof, rows, cols = guesses.shape
     steps = step_weight.shape[0]
     plan = Plan((planes, gx, gy), dof, rows, cols, steps)
-    half = lax.axis_index("gy").astype(jnp.int32)[None]
+    place = jnp.stack([lax.axis_index(name) for name in ("tm", "gx", "gy")]).astype(jnp.int32)
 
     start = lax.ppermute(guesses, "tm", earlier(planes))
-    edge_f, edge_g = edge_kernel(plan)(half, forcing, guesses, land_mask)
+    edge_f, edge_g = edge_kernel(plan)(place, forcing, guesses, land_mask)
     edge_f = lax.ppermute(edge_f, "gy", [(0, 1), (1, 0)])
     edge_g = lax.ppermute(
         edge_g,
         ("tm", "gy"),
         [(t * gy + c, (t - 1) * gy + 1 - c) for t in range(1, planes) for c in range(gy)],
     )
-    f_pieces = pack_kernel(plan, True)(half, forcing, edge_f, land_mask)
-    f_pieces = lax.all_to_all(f_pieces, "gx", 0, 0, tiled=True)
-    a_pieces = pack_kernel(plan, False)(half, start, edge_g)
-    a_pieces = lax.all_to_all(a_pieces, "gx", 0, 0, tiled=True)
-    relaxed = relax_kernel(plan, steps)(
-        step_weight, stacked_matrix(fine_matrix, coupling), f_pieces, a_pieces
-    )
-    relaxed = lax.all_to_all(relaxed, "gx", 0, 0, tiled=True)
-    residual = residual_kernel(plan)(relaxed, guesses, land_mask)
-
+    f_pieces = pack_kernel(plan, True)(place, forcing, edge_f, land_mask, guesses)
+    f_pieces = swapped(f_pieces, "gx")
+    a_pieces = swapped(pack_kernel(plan, False)(place, start, edge_g), "gx")
+    full = jnp.concatenate([fine_matrix[None], coupling], axis=0).reshape(-1, dof)
+    *relaxed, land_piece = relax_kernel(plan, steps)(
+        place, step_weight, split_matrix(full), *f_pieces, *a_pieces
+    )
+    home, across = relaxed[:gx], relaxed[gx:]
+    if plan.square:
+        across = swapped(across, "tm")
+        home = swapped(home, "gx")
+        residual, total = residual_kernel(plan)(place, guesses, *home)
+        parts = coarse_kernel(plan)(place, split_matrix(coarse_matrix), land_piece, *across)
+        parts = [
+            lax.ppermute(
+                parts[k],
+                ("tm", "gx"),
+                [(p * gx + i, (i ^ k) * gx + p) for p in range(planes) for i in range(gx)],
+            )
+            for k in range(gx)
+        ]
+        return update_kernel(plan)(place, total, *parts), residual
+
+    residual, total = residual_kernel(plan)(place, guesses, *swapped(home, "gx"))
     mask = land_mask.astype(F32)[None]
 
     def advance(field):
         moved = jnp.einsum("ij,jxy->ixy", coarse_matrix, field, precision=lax.Precision.HIGHEST)
-        return moved * mask + residual[0]
+        return moved * mask
 
     def turn(_, incoming):
-        return lax.ppermute(advance(incoming), "tm", earlier(planes))
+        return lax.ppermute(advance(incoming) + residual[0], "tm", earlier(planes))
 
     incoming = lax.fori_loop(0, planes - 1, turn, jnp.zeros_like(residual[0]))
-    return guesses + advance(incoming)[None], residual
+    return total + advance(incoming)[None], residual
 
 
 def solution(mesh):

time: 98.5 us -> 71.4 us (0.72)
  the two profiles are of different devices: /device:TPU:0 before, /device:TPU:2 now
where the time goes in v1:
time: 71.4 us; the launch traced here: 71 us
  starting transfers between devices  27.5 us (39%)
  Pallas kernels  24.5 us (34%)
  waiting for transfers between devices  16.6 us (23%)
  other arithmetic  0.91 us (1%)
  between operations  0.84 us (1%)
    pallas_call x7, Pallas kernels, placed(): run(*(arg if i in smem or i in hbm else pltpu.with_memory_space_constrain...  24.5 us
    ppermute x12, starting transfers between devices, swapped(): lax.ppermute(pieces[k], axis, [(i, i ^ k) for i in range(count)])  16.8 us
    ppermute x12, waiting for transfers between devices, swapped(): lax.ppermute(pieces[k], axis, [(i, i ^ k) for i in range(count)])  12.1 us
    ppermute x4, starting transfers between devices, per_device(): lax.ppermute(parts[k], ('tm', 'gx'), [(p * gx + i, (i ^ k) * gx + p) for...  8.08 us
    ppermute x4, waiting for transfers between devices, per_device(): lax.ppermute(parts[k], ('tm', 'gx'), [(p * gx + i, (i ^ k) * gx + p) for...  4.55 us
  transfers between devices with their start and end apart: 19, of which 9 were waited for; matrix products, arithmetic and copies ran while one was open for 1% of the time, Pallas kernels for 11%

profile of v1, /device:TPU:2, one launch (start us, length us, event | category | flops | bytes accessed | tf_op | source)
XLA Modules:
  0.0 71.0 jit_solution(3593300679493252125)
XLA Ops:
  0.6 1.3 %collective-permute-start.4 = (f32[1,64,8,128]{3,2,1,0:T(8,128)}, f32[1,64,8,128]{3,2,1,0:T(8,128)S(1)}, u32[]{:S(2)}, u32[]{:S(2)}) collective-permute-start(f32[1,64,8,128]{3,2,1,0:T(8,128)} %guess_ref.3), channel_id=1, source_target_pairs={{8,0},{16,8},{24,16},{9,1},{17,9},{25,17},{10,2},{18,10},{26,18},{... | collective-permute-start | bytes 786440 | tf_op jit(solution)/shard_map/ppermute | solution.py:441
  1.9 0.7 pad_add_fusion.place_ref
  2.6 0.0 copy-start.3
  2.6 0.0 copy-start.4
  2.6 0.0 copy-start.1
  2.6 1.4 %shard_map.86 = (f32[72,128]{1,0:T(8,128)S(1)}, f32[64,128]{1,0:T(8,128)S(1)}) custom-call(s32[3]{0:T(128)} %pad_add_fusion.place_ref, f32[1,64,8,128]{3,2,1,0:T(8,128)} %field_ref.1, f32[1,64,8,128]{3,2,1,0:T(8,128)} %guess_ref.3, s32[8,128]{1,0:T(8,128)} %rest_0_.1), custom_call_target="tpu_custom_call" | custom-call | tf_op jit(solution)/shard_map/pallas_call | solution.py:58
  4.0 0.0 copy-start
  4.1 0.1 collective-permute-start
  4.1 1.3 %collective-permute-start.5 = (f32[64,128]{1,0:T(8,128)S(1)}, f32[64,128]{1,0:T(8,128)S(1)}, u32[]{:S(2)}, u32[]{:S(2)}) collective-permute-start(f32[64,128]{1,0:T(8,128)S(1)} %get-tuple-element.32), channel_id=1, source_target_pairs={{8,1},{9,0},{16,9},{17,8},{24,17},{25,16},{10,3},{11,2},{18,11},{1... | collective-permute-start | bytes 98312 | tf_op jit(solution)/shard_map/ppermute | solution.py:444
  5.4 0.0 copy-done.3
  5.4 0.0 copy-done.4
  5.5 0.0 copy-start.2
  5.5 0.0 collective-permute-done.edge_ref
  5.5 0.0 copy-done.1
  5.5 0.0 copy-done
  5.5 0.6 copy-done.2
  6.1 1.7 %shard_map.87 = (f32[392,128]{1,0:T(8,128)S(1)}, f32[392,128]{1,0:T(8,128)S(1)}, f32[392,128]{1,0:T(8,128)S(1)}, f32[392,128]{1,0:T(8,128)S(1)}) custom-call(s32[3]{0:T(128)} %pad_add_fusion.place_ref, f32[1,64,8,128]{3,2,1,0:T(8,128)S(1)} %copy-done.1, f32[72,128]{1,0:T(8,128)S(1)} %collective-permute-done.edge_ref, s32[8,128]{1,0:T(8,128)S(1)} %copy-done.2, ...), custom_call_target="tpu_custom_call" | custom-call | tf_op jit(solution)/shard_map/pallas_call | solution.py:58
  7.9 0.1 collective-permute-start.1
  8.0 2.1 %collective-permute-start.2 = (f32[392,128]{1,0:T(8,128)S(1)}, f32[392,128]{1,0:T(8,128)S(1)}, u32[]{:S(2)}, u32[]{:S(2)}) collective-permute-start(f32[392,128]{1,0:T(8,128)S(1)} %get-tuple-element.30), channel_id=1, source_target_pairs={{0,4},{2,6},{4,0},{6,2},{1,5},{3,7},{5,1},{7,3},{8,12},{10,14},{12... | collective-permute-start | bytes 602120 | tf_op jit(solution)/shard_map/ppermute | solution.py:429
  10.1 0.0 copy-start.5
  10.1 1.4 %collective-permute-start.3 = (f32[392,128]{1,0:T(8,128)S(1)}, f32[392,128]{1,0:T(8,128)S(1)}, u32[]{:S(2)}, u32[]{:S(2)}) collective-permute-start(f32[392,128]{1,0:T(8,128)S(1)} %get-tuple-element.31), channel_id=1, source_target_pairs={{0,6},{2,4},{4,2},{6,0},{1,7},{3,5},{5,3},{7,1},{8,14},{10,12},{12... | collective-permute-start | bytes 602120 | tf_op jit(solution)/shard_map/ppermute | solution.py:429
  11.5 0.0 collective-permute-done.5.edge_ref
  11.5 0.0 collective-permute-done.4.field_ref
  11.5 1.3 %shard_map.88 = (f32[256,128]{1,0:T(8,128)S(1)}, f32[256,128]{1,0:T(8,128)S(1)}, f32[256,128]{1,0:T(8,128)S(1)}, f32[256,128]{1,0:T(8,128)S(1)}) custom-call(s32[3]{0:T(128)} %pad_add_fusion.place_ref, f32[1,64,8,128]{3,2,1,0:T(8,128)S(1)} %collective-permute-done.4.field_ref, f32[64,128]{1,0:T(8,128)S(1)} %collective-permute-done.5.edge_ref), custom_call_target="tpu_custom_call" | custom-call | tf_op jit(solution)/shard_map/pallas_call | solution.py:58
  12.8 0.2 collective-permute-start.6
  13.0 1.9 %collective-permute-start.7 = (f32[256,128]{1,0:T(8,128)S(1)}, f32[256,128]{1,0:T(8,128)S(1)}, u32[]{:S(2)}, u32[]{:S(2)}) collective-permute-start(f32[256,128]{1,0:T(8,128)S(1)} %get-tuple-element.35), channel_id=1, source_target_pairs={{0,4},{2,6},{4,0},{6,2},{1,5},{3,7},{5,1},{7,3},{8,12},{10,14},{12... | collective-permute-start | bytes 393224 | tf_op jit(solution)/shard_map/ppermute | solution.py:429
  15.0 0.8 %collective-permute-done.1.refs_1_ = f32[392,128]{1,0:T(8,128)S(1)} collective-permute-done((f32[392,128]{1,0:T(8,128)S(1)}, f32[392,128]{1,0:T(8,128)S(1)}, u32[]{:S(2)}, u32[]{:S(2)}) %collective-permute-start.1) | collective-permute-done | bytes 200736 | tf_op jit(solution)/shard_map/ppermute | solution.py:429
  15.8 1.5 %collective-permute-start.8 = (f32[256,128]{1,0:T(8,128)S(1)}, f32[256,128]{1,0:T(8,128)S(1)}, u32[]{:S(2)}, u32[]{:S(2)}) collective-permute-start(f32[256,128]{1,0:T(8,128)S(1)} %get-tuple-element.36), channel_id=1, source_target_pairs={{0,6},{2,4},{4,2},{6,0},{1,7},{3,5},{5,3},{7,1},{8,14},{10,12},{12... | collective-permute-start | bytes 393224 | tf_op jit(solution)/shard_map/ppermute | solution.py:429
  17.3 0.0 copy-done.5
  17.3 0.1 pad_maximum_fusion.1.matrix_ref
  17.4 2.0 %collective-permute-done.2.refs_2_ = f32[392,128]{1,0:T(8,128)S(1)} collective-permute-done((f32[392,128]{1,0:T(8,128)S(1)}, f32[392,128]{1,0:T(8,128)S(1)}, u32[]{:S(2)}, u32[]{:S(2)}) %collective-permute-start.2) | collective-permute-done | bytes 200736 | tf_op jit(solution)/shard_map/ppermute | solution.py:429
  19.4 1.7 %collective-permute-done.3.refs_3_ = f32[392,128]{1,0:T(8,128)S(1)} collective-permute-done((f32[392,128]{1,0:T(8,128)S(1)}, f32[392,128]{1,0:T(8,128)S(1)}, u32[]{:S(2)}, u32[]{:S(2)}) %collective-permute-start.3) | collective-permute-done | bytes 200736 | tf_op jit(solution)/shard_map/ppermute | solution.py:429
  21.1 1.8 %collective-permute-done.6.refs_5_ = f32[256,128]{1,0:T(8,128)S(1)} collective-permute-done((f32[256,128]{1,0:T(8,128)S(1)}, f32[256,128]{1,0:T(8,128)S(1)}, u32[]{:S(2)}, u32[]{:S(2)}) %collective-permute-start.6) | collective-permute-done | bytes 131104 | tf_op jit(solution)/shard_map/ppermute | solution.py:429
  23.0 1.7 %collective-permute-done.7.refs_6_ = f32[256,128]{1,0:T(8,128)S(1)} collective-permute-done((f32[256,128]{1,0:T(8,128)S(1)}, f32[256,128]{1,0:T(8,128)S(1)}, u32[]{:S(2)}, u32[]{:S(2)}) %collective-permute-start.7) | collective-permute-done | bytes 131104 | tf_op jit(solution)/shard_map/ppermute | solution.py:429
  24.7 1.6 %collective-permute-done.8.refs_7_ = f32[256,128]{1,0:T(8,128)S(1)} collective-permute-done((f32[256,128]{1,0:T(8,128)S(1)}, f32[256,128]{1,0:T(8,128)S(1)}, u32[]{:S(2)}, u32[]{:S(2)}) %collective-permute-start.8) | collective-permute-done | bytes 131104 | tf_op jit(solution)/shard_map/ppermute | solution.py:429
  26.2 15.3 %shard_map.89 = (f32[128,128]{1,0:T(8,128)S(1)}, f32[128,128]{1,0:T(8,128)S(1)}, f32[128,128]{1,0:T(8,128)S(1)}, f32[128,128]{1,0:T(8,128)S(1)}, f32[128,128]{1,...) custom-call(s32[3]{0:T(128)} %pad_add_fusion.place_ref, ...), custom_call_target="tpu_custom_call" | custom-call | tf_op jit(solution)/shard_map/pallas_call | solution.py:58
  41.6 3.3 %collective-permute-start.12 = (f32[128,128]{1,0:T(8,128)S(1)}, f32[128,128]{1,0:T(8,128)S(1)}, u32[]{:S(2)}, u32[]{:S(2)}) collective-permute-start(f32[128,128]{1,0:T(8,128)S(1)} %get-tuple-element.44), channel_id=1, source_target_pairs={{0,8},{8,0},{16,24},{24,16},{1,9},{9,1},{17,25},{25,17},{2,10},{10... | collective-permute-start | bytes 196616 | tf_op jit(solution)/shard_map/ppermute | solution.py:429
  44.9 2.7 %collective-permute-start.13 = (f32[128,128]{1,0:T(8,128)S(1)}, f32[128,128]{1,0:T(8,128)S(1)}, u32[]{:S(2)}, u32[]{:S(2)}) collective-permute-start(f32[128,128]{1,0:T(8,128)S(1)} %get-tuple-element.45), channel_id=1, source_target_pairs={{0,16},{8,24},{16,0},{24,8},{1,17},{9,25},{17,1},{25,9},{2,18},{10... | collective-permute-start | bytes 196616 | tf_op jit(solution)/shard_map/ppermute | solution.py:429
  47.6 0.0 collective-permute-start.14
  47.6 0.9 %collective-permute-start.10 = (f32[128,128]{1,0:T(8,128)S(1)}, f32[128,128]{1,0:T(8,128)S(1)}, u32[]{:S(2)}, u32[]{:S(2)}) collective-permute-start(f32[128,128]{1,0:T(8,128)S(1)} %get-tuple-element.39), channel_id=1, source_target_pairs={{0,4},{2,6},{4,0},{6,2},{1,5},{3,7},{5,1},{7,3},{8,12},{10,14},{12... | collective-permute-start | bytes 196616 | tf_op jit(solution)/shard_map/ppermute | solution.py:429
  48.4 1.4 %collective-permute-start.11 = (f32[128,128]{1,0:T(8,128)S(1)}, f32[128,128]{1,0:T(8,128)S(1)}, u32[]{:S(2)}, u32[]{:S(2)}) collective-permute-start(f32[128,128]{1,0:T(8,128)S(1)} %get-tuple-element.40), channel_id=1, source_target_pairs={{0,6},{2,4},{4,2},{6,0},{1,7},{3,5},{5,3},{7,1},{8,14},{10,12},{12... | collective-permute-start | bytes 196616 | tf_op jit(solution)/shard_map/ppermute | solution.py:429
  49.9 0.1 pad_maximum_fusion.2.matrix_ref
  50.0 0.0 collective-permute-done.12.refs_1_
  50.0 1.2 %collective-permute-start.9 = (f32[128,128]{1,0:T(8,128)S(1)}, f32[128,128]{1,0:T(8,128)S(1)}, u32[]{:S(2)}, u32[]{:S(2)}) collective-permute-start(f32[128,128]{1,0:T(8,128)S(1)} %get-tuple-element.38), channel_id=1, source_target_pairs={{0,2},{2,0},{4,6},{6,4},{1,3},{3,1},{5,7},{7,5},{8,10},{10,8},{12,... | collective-permute-start | bytes 196616 | tf_op jit(solution)/shard_map/ppermute | solution.py:429
  51.2 0.7 %collective-permute-done.13.refs_2_ = f32[128,128]{1,0:T(8,128)S(1)} collective-permute-done((f32[128,128]{1,0:T(8,128)S(1)}, f32[128,128]{1,0:T(8,128)S(1)}, u32[]{:S(2)}, u32[]{:S(2)}) %collective-permute-start.13) | collective-permute-done | bytes 65568 | tf_op jit(solution)/shard_map/ppermute | solution.py:429
  52.0 1.7 %collective-permute-done.14.refs_3_ = f32[128,128]{1,0:T(8,128)S(1)} collective-permute-done((f32[128,128]{1,0:T(8,128)S(1)}, f32[128,128]{1,0:T(8,128)S(1)}, u32[]{:S(2)}, u32[]{:S(2)}) %collective-permute-start.14) | collective-permute-done | bytes 65568 | tf_op jit(solution)/shard_map/ppermute | solution.py:429
  53.6 1.1 %shard_map.91 = (f32[128,128]{1,0:T(8,128)S(1)}, f32[128,128]{1,0:T(8,128)S(1)}, f32[128,128]{1,0:T(8,128)S(1)}, f32[128,128]{1,0:T(8,128)S(1)}) custom-call(s32[3]{0:T(128)} %pad_add_fusion.place_ref, bf16[64,192]{1,0:T(8,128)(2,1)S(1)} %pad_maximum_fusion.2.matrix_ref, f32[16,128]{1,0:T(8,128)S(1)} %get-tuple-element.42.land_ref, ...), custom_call_target="tpu_custom_call" | custom-call | tf_op jit(solution)/shard_map/pallas_call | solution.py:58
  54.8 1.9 %collective-permute-start.15 = (f32[128,128]{1,0:T(8,128)S(1)}, f32[128,128]{1,0:T(8,128)S(1)}, u32[]{:S(2)}, u32[]{:S(2)}) collective-permute-start(f32[128,128]{1,0:T(8,128)S(1)} %get-tuple-element.47), channel_id=1, source_target_pairs={{0,0},{2,8},{4,16},{6,24},{8,2},{10,10},{12,18},{14,26},{16,4},{18... | collective-permute-start | bytes 196616 | tf_op jit(solution)/shard_map/ppermute | solution.py:463
  56.7 0.1 collective-permute-start.16
  56.8 0.0 collective-permute-done.10.refs_2_
  56.8 6.1 %collective-permute-start.17 = (f32[128,128]{1,0:T(8,128)S(1)}, f32[128,128]{1,0:T(8,128)S(1)}, u32[]{:S(2)}, u32[]{:S(2)}) collective-permute-start(f32[128,128]{1,0:T(8,128)S(1)} %get-tuple-element.49), channel_id=1, source_target_pairs={{0,16},{2,24},{4,0},{6,8},{8,18},{10,26},{12,2},{14,10},{16,20},{1... | collective-permute-start | bytes 196616 | tf_op jit(solution)/shard_map/ppermute | solution.py:463
  62.9 0.0 collective-permute-done.11.refs_3_
  62.9 0.0 collective-permute-start.18
  62.9 0.0 collective-permute-done.9.refs_1_
  62.9 1.9 %shard_map.90 = (f32[1,64,8,128]{3,2,1,0:T(8,128)}, f32[1,64,8,128]{3,2,1,0:T(8,128)S(1)}) custom-call(s32[3]{0:T(128)} %pad_add_fusion.place_ref, f32[1,64,8,128]{3,2,1,0:T(8,128)S(1)} %copy-done, f32[128,128]{1,0:T(8,128)S(1)} %get-tuple-element.37.refs_0_, f32[128,128]{1,0:T(8,128)S(1)} %collective-permute-done.9.refs_1_, ...), custom_call_target="tpu_custom_call" | custom-call | tf_op jit(solution)/shard_map/pallas_call | solution.py:58
  64.8 0.0 collective-permute-done.15.refs_0_
  64.8 0.0 collective-permute-done.16.refs_1_
  64.8 0.0 collective-permute-done.17.refs_2_
  64.8 4.5 %collective-permute-done.18.refs_3_ = f32[128,128]{1,0:T(8,128)S(1)} collective-permute-done((f32[128,128]{1,0:T(8,128)S(1)}, f32[128,128]{1,0:T(8,128)S(1)}, u32[]{:S(2)}, u32[]{:S(2)}) %collective-permute-start.18) | collective-permute-done | bytes 65568 | tf_op jit(solution)/shard_map/ppermute | solution.py:463
  69.3 1.7 %shard_map.92 = f32[1,64,8,128]{3,2,1,0:T(8,128)} custom-call(s32[3]{0:T(128)} %pad_add_fusion.place_ref, f32[1,64,8,128]{3,2,1,0:T(8,128)S(1)} %get-tuple-element.41.sum_ref, f32[128,128]{1,0:T(8,128)S(1)} %collective-permute-done.15.refs_0_, f32[128,128]{1,0:T(8,128)S(1)} %collective-permute-done.16.refs_1_, ...), custom_call_target="tpu_custom_call" | custom-call | tf_op jit(solution)/shard_map/pallas_call | solution.py:58
  (3 shorter events, 0.1 us)
Async XLA Ops:
  0.6 10.9 %collective-permute-start.4 = (f32[1,64,8,128]{3,2,1,0:T(8,128)}, f32[1,64,8,128]{3,2,1,0:T(8,128)S(1)}, u32[]{:S(2)}, u32[]{:S(2)}) collective-permute-start(f32[1,64,8,128]{3,2,1,0:T(8,128)} %guess_ref.3), channel_id=1, source_target_pairs={{8,0},{16,8},{24,16},{9,1},{17,9},{25,17},{10,2},{18,10},{26,18},{... | collective-permute-start | bytes 786440 | tf_op jit(solution)/shard_map/ppermute | solution.py:441
  2.6 2.8 %copy-start.3 = (f32[4,64,64]{2,1,0:T(8,128)S(1)}, f32[4,64,64]{2,1,0:T(8,128)}, u32[]{:S(2)}) copy-start(f32[4,64,64]{2,1,0:T(8,128)} %param.12) | copy-start | bytes 196612
  2.6 2.8 %copy-start.4 = (f32[64,64]{1,0:T(8,128)S(1)}, f32[64,64]{1,0:T(8,128)}, u32[]{:S(2)}) copy-start(f32[64,64]{1,0:T(8,128)} %param.11) | copy-start | bytes 49156
  2.6 2.9 %copy-start.1 = (f32[1,64,8,128]{3,2,1,0:T(8,128)S(1)}, f32[1,64,8,128]{3,2,1,0:T(8,128)}, u32[]{:S(2)}) copy-start(f32[1,64,8,128]{3,2,1,0:T(8,128)} %field_ref.1) | copy-start | bytes 786436
  4.0 1.5 %copy-start = (f32[1,64,8,128]{3,2,1,0:T(8,128)S(1)}, f32[1,64,8,128]{3,2,1,0:T(8,128)}, u32[]{:S(2)}) copy-start(f32[1,64,8,128]{3,2,1,0:T(8,128)} %guess_ref.3) | copy-start | bytes 786436
  4.1 1.4 %collective-permute-start = (f32[72,128]{1,0:T(8,128)S(1)}, f32[72,128]{1,0:T(8,128)S(1)}, u32[]{:S(2)}, u32[]{:S(2)}) collective-permute-start(f32[72,128]{1,0:T(8,128)S(1)} %get-tuple-element.27), channel_id=1, source_target_pairs={{0,1},{1,0},{2,3},{3,2},{4,5},{5,4},{6,7},{7,6},{8,9},{9,8},{10,11... | collective-permute-start | bytes 110600 | tf_op jit(solution)/shard_map/ppermute | solution.py:443
  4.1 7.4 %collective-permute-start.5 = (f32[64,128]{1,0:T(8,128)S(1)}, f32[64,128]{1,0:T(8,128)S(1)}, u32[]{:S(2)}, u32[]{:S(2)}) collective-permute-start(f32[64,128]{1,0:T(8,128)S(1)} %get-tuple-element.32), channel_id=1, source_target_pairs={{8,1},{9,0},{16,9},{17,8},{24,17},{25,16},{10,3},{11,2},{18,11},{1... | collective-permute-start | bytes 98312 | tf_op jit(solution)/shard_map/ppermute | solution.py:444
  5.5 0.7 copy-start.2
  7.9 7.9 %collective-permute-start.1 = (f32[392,128]{1,0:T(8,128)S(1)}, f32[392,128]{1,0:T(8,128)S(1)}, u32[]{:S(2)}, u32[]{:S(2)}) collective-permute-start(f32[392,128]{1,0:T(8,128)S(1)} %get-tuple-element.29), channel_id=1, source_target_pairs={{0,2},{2,0},{4,6},{6,4},{1,3},{3,1},{5,7},{7,5},{8,10},{10,8},{12,... | collective-permute-start | bytes 602120 | tf_op jit(solution)/shard_map/ppermute | solution.py:429
  8.0 11.4 %collective-permute-start.2 = (f32[392,128]{1,0:T(8,128)S(1)}, f32[392,128]{1,0:T(8,128)S(1)}, u32[]{:S(2)}, u32[]{:S(2)}) collective-permute-start(f32[392,128]{1,0:T(8,128)S(1)} %get-tuple-element.30), channel_id=1, source_target_pairs={{0,4},{2,6},{4,0},{6,2},{1,5},{3,7},{5,1},{7,3},{8,12},{10,14},{12... | collective-permute-start | bytes 602120 | tf_op jit(solution)/shard_map/ppermute | solution.py:429
  10.1 7.2 %copy-start.5 = (f32[64,64]{1,0:T(8,128)S(1)}, f32[64,64]{1,0:T(8,128)}, u32[]{:S(2)}) copy-start(f32[64,64]{1,0:T(8,128)} %param.13) | copy-start | bytes 49156
  10.1 11.0 %collective-permute-start.3 = (f32[392,128]{1,0:T(8,128)S(1)}, f32[392,128]{1,0:T(8,128)S(1)}, u32[]{:S(2)}, u32[]{:S(2)}) collective-permute-start(f32[392,128]{1,0:T(8,128)S(1)} %get-tuple-element.31), channel_id=1, source_target_pairs={{0,6},{2,4},{4,2},{6,0},{1,7},{3,5},{5,3},{7,1},{8,14},{10,12},{12... | collective-permute-start | bytes 602120 | tf_op jit(solution)/shard_map/ppermute | solution.py:429
  12.8 10.1 %collective-permute-start.6 = (f32[256,128]{1,0:T(8,128)S(1)}, f32[256,128]{1,0:T(8,128)S(1)}, u32[]{:S(2)}, u32[]{:S(2)}) collective-permute-start(f32[256,128]{1,0:T(8,128)S(1)} %get-tuple-element.34), channel_id=1, source_target_pairs={{0,2},{2,0},{4,6},{6,4},{1,3},{3,1},{5,7},{7,5},{8,10},{10,8},{12,... | collective-permute-start | bytes 393224 | tf_op jit(solution)/shard_map/ppermute | solution.py:429
  13.0 11.6 %collective-permute-start.7 = (f32[256,128]{1,0:T(8,128)S(1)}, f32[256,128]{1,0:T(8,128)S(1)}, u32[]{:S(2)}, u32[]{:S(2)}) collective-permute-start(f32[256,128]{1,0:T(8,128)S(1)} %get-tuple-element.35), channel_id=1, source_target_pairs={{0,4},{2,6},{4,0},{6,2},{1,5},{3,7},{5,1},{7,3},{8,12},{10,14},{12... | collective-permute-start | bytes 393224 | tf_op jit(solution)/shard_map/ppermute | solution.py:429
  15.8 10.4 %collective-permute-start.8 = (f32[256,128]{1,0:T(8,128)S(1)}, f32[256,128]{1,0:T(8,128)S(1)}, u32[]{:S(2)}, u32[]{:S(2)}) collective-permute-start(f32[256,128]{1,0:T(8,128)S(1)} %get-tuple-element.36), channel_id=1, source_target_pairs={{0,6},{2,4},{4,2},{6,0},{1,7},{3,5},{5,3},{7,1},{8,14},{10,12},{12... | collective-permute-start | bytes 393224 | tf_op jit(solution)/shard_map/ppermute | solution.py:429
  41.6 8.4 %collective-permute-start.12 = (f32[128,128]{1,0:T(8,128)S(1)}, f32[128,128]{1,0:T(8,128)S(1)}, u32[]{:S(2)}, u32[]{:S(2)}) collective-permute-start(f32[128,128]{1,0:T(8,128)S(1)} %get-tuple-element.44), channel_id=1, source_target_pairs={{0,8},{8,0},{16,24},{24,16},{1,9},{9,1},{17,25},{25,17},{2,10},{10... | collective-permute-start | bytes 196616 | tf_op jit(solution)/shard_map/ppermute | solution.py:429
  44.9 7.1 %collective-permute-start.13 = (f32[128,128]{1,0:T(8,128)S(1)}, f32[128,128]{1,0:T(8,128)S(1)}, u32[]{:S(2)}, u32[]{:S(2)}) collective-permute-start(f32[128,128]{1,0:T(8,128)S(1)} %get-tuple-element.45), channel_id=1, source_target_pairs={{0,16},{8,24},{16,0},{24,8},{1,17},{9,25},{17,1},{25,9},{2,18},{10... | collective-permute-start | bytes 196616 | tf_op jit(solution)/shard_map/ppermute | solution.py:429
  47.6 6.1 %collective-permute-start.14 = (f32[128,128]{1,0:T(8,128)S(1)}, f32[128,128]{1,0:T(8,128)S(1)}, u32[]{:S(2)}, u32[]{:S(2)}) collective-permute-start(f32[128,128]{1,0:T(8,128)S(1)} %get-tuple-element.46), channel_id=1, source_target_pairs={{0,24},{8,16},{16,8},{24,0},{1,25},{9,17},{17,9},{25,1},{2,26},{10... | collective-permute-start | bytes 196616 | tf_op jit(solution)/shard_map/ppermute | solution.py:429
  47.6 9.2 %collective-permute-start.10 = (f32[128,128]{1,0:T(8,128)S(1)}, f32[128,128]{1,0:T(8,128)S(1)}, u32[]{:S(2)}, u32[]{:S(2)}) collective-permute-start(f32[128,128]{1,0:T(8,128)S(1)} %get-tuple-element.39), channel_id=1, source_target_pairs={{0,4},{2,6},{4,0},{6,2},{1,5},{3,7},{5,1},{7,3},{8,12},{10,14},{12... | collective-permute-start | bytes 196616 | tf_op jit(solution)/shard_map/ppermute | solution.py:429
  48.4 14.4 %collective-permute-start.11 = (f32[128,128]{1,0:T(8,128)S(1)}, f32[128,128]{1,0:T(8,128)S(1)}, u32[]{:S(2)}, u32[]{:S(2)}) collective-permute-start(f32[128,128]{1,0:T(8,128)S(1)} %get-tuple-element.40), channel_id=1, source_target_pairs={{0,6},{2,4},{4,2},{6,0},{1,7},{3,5},{5,3},{7,1},{8,14},{10,12},{12... | collective-permute-start | bytes 196616 | tf_op jit(solution)/shard_map/ppermute | solution.py:429
  50.0 12.9 %collective-permute-start.9 = (f32[128,128]{1,0:T(8,128)S(1)}, f32[128,128]{1,0:T(8,128)S(1)}, u32[]{:S(2)}, u32[]{:S(2)}) collective-permute-start(f32[128,128]{1,0:T(8,128)S(1)} %get-tuple-element.38), channel_id=1, source_target_pairs={{0,2},{2,0},{4,6},{6,4},{1,3},{3,1},{5,7},{7,5},{8,10},{10,8},{12,... | collective-permute-start | bytes 196616 | tf_op jit(solution)/shard_map/ppermute | solution.py:429
  54.8 10.0 %collective-permute-start.15 = (f32[128,128]{1,0:T(8,128)S(1)}, f32[128,128]{1,0:T(8,128)S(1)}, u32[]{:S(2)}, u32[]{:S(2)}) collective-permute-start(f32[128,128]{1,0:T(8,128)S(1)} %get-tuple-element.47), channel_id=1, source_target_pairs={{0,0},{2,8},{4,16},{6,24},{8,2},{10,10},{12,18},{14,26},{16,4},{18... | collective-permute-start | bytes 196616 | tf_op jit(solution)/shard_map/ppermute | solution.py:463
  56.7 8.1 %collective-permute-start.16 = (f32[128,128]{1,0:T(8,128)S(1)}, f32[128,128]{1,0:T(8,128)S(1)}, u32[]{:S(2)}, u32[]{:S(2)}) collective-permute-start(f32[128,128]{1,0:T(8,128)S(1)} %get-tuple-element.48), channel_id=1, source_target_pairs={{0,8},{2,0},{4,24},{6,16},{8,10},{10,2},{12,26},{14,18},{16,12},{1... | collective-permute-start | bytes 196616 | tf_op jit(solution)/shard_map/ppermute | solution.py:463
  56.8 8.0 %collective-permute-start.17 = (f32[128,128]{1,0:T(8,128)S(1)}, f32[128,128]{1,0:T(8,128)S(1)}, u32[]{:S(2)}, u32[]{:S(2)}) collective-permute-start(f32[128,128]{1,0:T(8,128)S(1)} %get-tuple-element.49), channel_id=1, source_target_pairs={{0,16},{2,24},{4,0},{6,8},{8,18},{10,26},{12,2},{14,10},{16,20},{1... | collective-permute-start | bytes 196616 | tf_op jit(solution)/shard_map/ppermute | solution.py:463
  62.9 6.4 %collective-permute-start.18 = (f32[128,128]{1,0:T(8,128)S(1)}, f32[128,128]{1,0:T(8,128)S(1)}, u32[]{:S(2)}, u32[]{:S(2)}) collective-permute-start(f32[128,128]{1,0:T(8,128)S(1)} %get-tuple-element.50), channel_id=1, source_target_pairs={{0,24},{2,16},{4,8},{6,0},{8,26},{10,18},{12,10},{14,2},{16,28},{1... | collective-permute-start | bytes 196616 | tf_op jit(solution)/shard_map/ppermute | solution.py:463
